TPU v7x, 32 devices: a whole 2x2x4 slice. The times are simulated.
32 devices in a mesh: fiber: 8 (over z, x), seg: 4 (over y, core).
Axes of the slice: x: 2, y: 2, z: 4, core: 2. Of those that a mesh axis runs over, the one named last changes fastest.
Arguments:
- raw_strain: bfloat16 [64, 1024, 2048], P('seg', 'fiber'), may hold values from -6 to 6
- fir_taps: float32 [31], replicated, may hold values from -1 to 1
- good_mask: int32 [64, 1024], P('seg', 'fiber'), may hold values from 0 to 1, as said below
Outputs:
- stacked_spectra: float32 [144, 1024, 2, 128], P('seg', 'fiber')
Inputs may be any that keep to these rules, and one draw needn't show every extreme that they name: `good_mask`: 0 or 1; some channels are 0 in every segment.
All inputs are finite; a program needn't handle non-finite values.
Results may differ from a plain program's by a relative error of at most 0.005.
Values may be sent and summed in bfloat16 or wider, within the bound.
A program may use at most 192 MiB of HBM per device.

v0:
```python
import functools
import math

import jax
import jax.numpy as jnp
import numpy as np
from jax import lax
from jax.experimental import pallas as pl
from jax.experimental.pallas import tpu as pltpu
from jax.sharding import PartitionSpec as P

NF = 144
LOW = 16
SMOOTH = 4
LAGS = 128
EDGE = 16

epsilon = 1e-06
water_share = 0.1
MESH = pl.DeviceIdType.MESH
VMEM_LIMIT = 40 * 2**20


def row_bins(shares):
    per = NF // shares
    return np.concatenate([np.tile(np.arange(k * per, (k + 1) * per), 2) for k in range(shares)])


def row_parts(shares):
    per = NF // shares
    return np.tile(np.repeat(np.arange(2), per), shares)


def dft_rows(samples, shares):
    bins, parts = row_bins(shares), row_parts(shares)
    index = ((bins[:, None] + LOW) * np.arange(samples)[None, :]) % samples
    angles = index.astype(np.float64) * (2.0 * math.pi / samples)
    return np.where(parts[:, None] == 0, np.cos(angles), -np.sin(angles)).astype(jnp.bfloat16)


def smooth_rows(shares):
    bins = row_bins(shares)
    return (np.abs(bins[:, None] - bins[None, :]) <= SMOOTH).astype(jnp.bfloat16)


def two_terms(x):
    hi = x.astype(jnp.bfloat16)
    return hi, (x - hi.astype(jnp.float32)).astype(jnp.bfloat16)


def mm(a, b):
    return jnp.dot(a, b, preferred_element_type=jnp.float32)


def mm_t(a, b):
    return lax.dot_general(a, b, (((1,), (1,)), ((), ())), preferred_element_type=jnp.float32)


def turned(x, shift):
    return pltpu.roll(x, shift, 1) if shift else x


def partner(seg, m):
    bit = 1
    while bit <= m:
        if m & bit:
            seg = seg + bit - 2 * bit * (seg // bit % 2)
        bit *= 2
    return seg


def taken(ref, q):
    shares, chunks, _, size, channels = ref.shape
    return ref[:, :, q].reshape(shares * chunks * size, channels)


def spectra_kernel(
    fibers, shares, taps_hbm, raw_ref, mask_ref, basis_hbm, smooth_hbm,
    own_ref, next_ref, part_ref, turn_ref,
    taps_ref, raw_v, edge_v, basis_ref, smooth_ref, flag_v, spec_v, out_l, out_r, in_l, in_r, band_v, mask_v,
    white_v, send_v,
    raw_sem, edge_sem, misc_sem, halo_send, halo_recv, own_send, own_recv, next_send, next_recv, local_sem,
):
    fib = lax.axis_index("fiber")
    seg = lax.axis_index("seg")
    segs, channels, _ = raw_ref.shape
    rows = basis_ref.shape[0]
    per = rows // shares
    taps = taps_ref.shape[0]
    half = (taps - 1) // 2
    has_prev = fib > 0
    has_next = fib < fibers - 1
    prev = jnp.maximum(fib - 1, 0)
    following = jnp.minimum(fib + 1, fibers - 1)
    size = channels // EDGE
    chunks = segs // size
    pairs = segs // 2
    chunk_pairs = size // 2

    taps_copy = pltpu.make_async_copy(taps_hbm, taps_ref, misc_sem.at[3])
    taps_copy.start()
    basis_copy = pltpu.make_async_copy(basis_hbm, basis_ref, misc_sem.at[0])
    basis_copy.start()
    edge_copies = [
        [
            pltpu.make_async_copy(
                raw_ref.at[pl.ds(c * size, size), pl.ds(start, EDGE), :],
                edge_v.at[c, i], edge_sem.at[2 * c + i],
            )
            for i, start in enumerate((0, channels - EDGE))
        ]
        for c in range(chunks)
    ]
    for copy in edge_copies[0]:
        copy.start()
    mask_copy = pltpu.make_async_copy(mask_ref, flag_v, misc_sem.at[2])
    mask_copy.start()
    raw_copies = [
        pltpu.make_async_copy(raw_ref.at[pl.ds(2 * p, 2)], raw_v.at[p], raw_sem.at[p])
        for p in range(pairs)
    ]
    for p, copy in enumerate(raw_copies):
        copy.start()
        if (p + 1) % chunk_pairs == 0 and (p + 1) // chunk_pairs < chunks:
            for edge in edge_copies[(p + 1) // chunk_pairs]:
                edge.start()
    smooth_copy = pltpu.make_async_copy(smooth_hbm, smooth_ref, misc_sem.at[1])
    smooth_copy.start()

    barrier = pltpu.get_barrier_semaphore()
    for m in range(1, shares):
        pl.semaphore_signal(
            barrier, inc=1, device_id=(fib, partner(seg, m)), device_id_type=MESH
        )
    @pl.when(has_prev)
    def _():
        pl.semaphore_signal(barrier, inc=1, device_id=(fib - 1, seg), device_id_type=MESH)
    @pl.when(has_next)
    def _():
        pl.semaphore_signal(barrier, inc=1, device_id=(fib + 1, seg), device_id_type=MESH)

    row = lax.broadcasted_iota(jnp.int32, (2 * channels, channels), 0)
    col = lax.broadcasted_iota(jnp.int32, (2 * channels, channels), 1)
    left = row - channels - EDGE
    right = row - EDGE
    place = jnp.where(row < channels, row, jnp.where(left < 0, left, right))
    place = jnp.where(row < channels + 2 * EDGE, place, 8 * channels)
    tap = place - col + half
    band = jnp.zeros((2 * channels, channels), jnp.float32)
    taps_copy.wait()
    for j in range(taps):
        band = jnp.where(tap == j, taps_ref[j], band)
    band_hi, band_lo = two_terms(band)
    band_v[:, :channels] = band_hi
    band_v[:, channels:] = band_lo

    @pl.when(jnp.logical_not(has_prev))
    def _():
        in_l[...] = jnp.zeros_like(in_l)
    @pl.when(jnp.logical_not(has_next))
    def _():
        in_r[...] = jnp.zeros_like(in_r)
        next_ref[...] = jnp.zeros_like(next_ref)

    def transform_edges(c):
        for copy in edge_copies[c]:
            copy.wait()
        ends = mm_t(basis_ref[...], edge_v[c].reshape(2 * channels, -1)).astype(jnp.bfloat16)
        out_l[c] = ends[:, :channels]
        out_r[c] = ends[:, channels:]

    basis_copy.wait()
    transform_edges(0)
    sides = (fib + fibers - 1) // fibers + (2 * fibers - 2 - fib) // fibers
    pl.semaphore_wait(barrier, shares - 1 + sides)

    to_prev = [
        pltpu.make_async_remote_copy(
            src_ref=out_l.at[c], dst_ref=in_r.at[c],
            send_sem=halo_send.at[0, c], recv_sem=halo_recv.at[0, c],
            device_id=(prev, seg), device_id_type=MESH,
        )
        for c in range(chunks)
    ]
    to_next = [
        pltpu.make_async_remote_copy(
            src_ref=out_r.at[c], dst_ref=in_l.at[c],
            send_sem=halo_send.at[1, c], recv_sem=halo_recv.at[1, c],
            device_id=(following, seg), device_id_type=MESH,
        )
        for c in range(chunks)
    ]
    def send_edges(c):
        @pl.when(has_prev)
        def _():
            to_prev[c].start()
        @pl.when(has_next)
        def _():
            to_next[c].start()

    send_edges(0)
    mask_copy.wait()
    mask_v[...] = flag_v[...].astype(jnp.float32)
    for c in range(chunks):
        flags = mask_v[c * size : (c + 1) * size, :].astype(jnp.bfloat16)
        for k in range(shares):
            send_v[k, c, per] = flags

    lane = lax.broadcasted_iota(jnp.int32, (rows, channels), 1)

    def transform(c):
        for p in range(c * chunk_pairs, (c + 1) * chunk_pairs):
            raw_copies[p].wait()
            spec_v[p] = mm_t(basis_ref[...], raw_v[p].reshape(2 * channels, -1))

    def whiten(c):
        def whiten_pair(i, carry):
            p = c * chunk_pairs + i
            lefts = in_l[c].astype(jnp.float32)
            rights = in_r[c].astype(jnp.float32)
            parts = []
            for h in range(2):
                slot = 2 * i + h
                l_roll = (channels - slot * EDGE) % channels
                r_roll = (channels + EDGE - slot * EDGE) % channels
                edges = jnp.where(lane < EDGE, turned(lefts, l_roll), turned(rights, r_roll))
                hi, lo = two_terms(spec_v[p, :, h * channels : (h + 1) * channels])
                wide = mm(jnp.concatenate([hi, edges.astype(jnp.bfloat16)], axis=1), band_v[...])
                parts.append(
                    wide[:, :channels] + wide[:, channels:] + mm(lo, band_v[:channels, :channels])
                )
            filtered = jnp.concatenate(parts, axis=1)
            power = filtered * filtered
            smooth = mm(smooth_ref[...], power.astype(jnp.bfloat16))
            total = jnp.sum(power, axis=0, keepdims=True)
            level = smooth * (1.0 / (2 * SMOOTH + 1)) + (total * (water_share / NF) + epsilon)
            good = jnp.concatenate(
                [mask_v[pl.ds(2 * p, 1), :], mask_v[pl.ds(2 * p + 1, 1), :]], axis=1
            )
            white = filtered * (lax.rsqrt(level) * good)
            white_v[pl.ds(2 * i, rows, size), :] = white[:, :channels]
            white_v[pl.ds(2 * i + 1, rows, size), :] = white[:, channels:]
            return carry

        for i in range(chunk_pairs):
            whiten_pair(i, 0)
        for k in range(shares):
            send_v[k, c, :per] = (
                white_v[k * per * size : (k + 1) * per * size, :]
                .reshape(per, size, channels)
                .astype(jnp.bfloat16)
            )

    def to_own(c, m):
        other = partner(seg, m)
        return pltpu.make_async_remote_copy(
            src_ref=send_v.at[other, c], dst_ref=own_ref.at[seg, c],
            send_sem=own_send.at[c, m], recv_sem=own_recv.at[c, m],
            device_id=(fib, other), device_id_type=MESH,
        )

    def from_own(c, m):
        other = partner(seg, m)
        return pltpu.make_async_remote_copy(
            src_ref=send_v.at[other, c], dst_ref=own_ref.at[other, c],
            send_sem=own_send.at[c, m], recv_sem=own_recv.at[c, m],
            device_id=(fib, other), device_id_type=MESH,
        )

    def hand_on(c, m):
        source = partner(seg, m)
        block = send_v if m == 0 else own_ref
        return pltpu.make_async_remote_copy(
            src_ref=block.at[source, c], dst_ref=next_ref.at[source, c],
            send_sem=next_send.at[c, m], recv_sem=next_recv.at[c, m],
            device_id=(prev, seg), device_id_type=MESH,
        )

    def kept(c):
        return pltpu.make_async_copy(send_v.at[seg, c], own_ref.at[seg, c], local_sem.at[c])

    def give(c):
        @pl.when(has_prev)
        def _():
            hand_on(c, 0).start()
        for m in range(1, shares):
            to_own(c, m).start()
        kept(c).start()

    def relay(c, m):
        from_own(c, m).wait_recv()
        @pl.when(has_prev)
        def _():
            hand_on(c, m).start()

    smooth_copy.wait()
    waiting = []
    for c in range(chunks):
        transform(c)
        if c + 1 < chunks:
            transform_edges(c + 1)
            send_edges(c + 1)
        if waiting:
            relay(*waiting.pop(0))
        @pl.when(has_prev)
        def _():
            to_next[c].wait_recv()
        @pl.when(has_next)
        def _():
            to_prev[c].wait_recv()
        whiten(c)
        give(c)
        waiting += [(c, m) for m in range(1, shares)]
    for item in waiting:
        relay(*item)
    for c in range(chunks):
        kept(c).wait()

    bins = per // 2
    group = next(n for n in (6, 4, 3, 2, 1) if bins % n == 0)

    def own_products(i, carry):
        for b in range(group):
            f = i * group + b
            re, im = taken(own_ref, f), taken(own_ref, bins + f)
            turned_left = jnp.concatenate([re, im], axis=0).T
            right = jnp.concatenate(
                [jnp.concatenate([re, im], axis=1), jnp.concatenate([im, -re], axis=1)], axis=0
            )
            turn_ref[f] = turned_left
            part_ref[f] = mm(turned_left, right)
        return carry

    lax.fori_loop(0, bins // group, own_products, 0)
    for c in range(chunks):
        for m in range(1, shares):
            to_own(c, m).wait_send()
    @pl.when(has_prev)
    def _():
        for c in range(chunks):
            to_prev[c].wait_send()
            for m in range(shares):
                hand_on(c, m).wait_send()
    @pl.when(has_next)
    def _():
        for c in range(chunks):
            to_next[c].wait_send()
            for m in range(shares):
                hand_on(c, m).wait_recv()


def cross_kernel(step_bins, own_ref, next_ref, part_ref, turn_ref, out_ref, scale_v):
    i = pl.program_id(0)
    shares, chunks, rows, size, channels = own_ref.shape
    bins = (rows - 1) // 2
    row = lax.broadcasted_iota(jnp.int32, (channels, channels), 0)
    col = lax.broadcasted_iota(jnp.int32, (channels, channels), 1)

    lags = (col + row + 1) % channels

    def lagged(near, far):
        chosen = jnp.where(col > row, near, far)
        return jnp.take_along_axis(chosen, lags, axis=1)

    def grams(a, b):
        return lax.dot_general(a, b, (((0,), (0,)), ((), ())), preferred_element_type=jnp.float32)

    @pl.when(i == 0)
    def _():
        here = taken(own_ref, rows - 1)
        counts = lagged(grams(here, here), grams(here, taken(next_ref, rows - 1)))
        scale_v[...] = 1.0 / jnp.maximum(counts, 1.0)

    scale = scale_v[...]
    for b in range(step_bins):
        f = i * step_bins + b
        re, im = taken(next_ref, f), taken(next_ref, bins + f)
        right = jnp.concatenate(
            [jnp.concatenate([re, im], axis=1), jnp.concatenate([im, -re], axis=1)], axis=0
        )
        far = mm(turn_ref[f], right)
        for n in range(2):
            cells = slice(n * channels, (n + 1) * channels)
            out_ref[b, pl.ds(n, channels, 2), :] = lagged(part_ref[f, :, cells], far[:, cells]) * scale


def on_device(raw_strain, fir_taps, good_mask):
    segs, channels, samples = raw_strain.shape
    fibers, shares = lax.axis_size("fiber"), lax.axis_size("seg")
    rows = 2 * NF
    per = rows // shares
    size = channels // EDGE
    chunks = segs // size
    block = jax.ShapeDtypeStruct((shares, chunks, per + 1, size, channels), jnp.bfloat16)
    vmem = pl.BlockSpec(memory_space=pltpu.VMEM)
    hbm = pl.BlockSpec(memory_space=pltpu.HBM)
    edges = pltpu.VMEM((chunks, rows, size * EDGE), jnp.bfloat16)
    basis, smooth = dft_rows(samples, shares), smooth_rows(shares)
    dma = pltpu.SemaphoreType.DMA
    spectral = pl.pallas_call(
        functools.partial(spectra_kernel, fibers, shares),
        out_shape=(
            block,
            block,
            jax.ShapeDtypeStruct((per // 2, channels, 2 * channels), jnp.float32),
            jax.ShapeDtypeStruct((per // 2, channels, 2 * shares * segs), jnp.bfloat16),
        ),
        in_specs=[hbm] * 5,
        out_specs=(vmem,) * 4,
        scratch_shapes=[
            pltpu.SMEM(fir_taps.shape, jnp.float32),
            pltpu.VMEM((segs // 2, 2, channels, samples), jnp.bfloat16),
            pltpu.VMEM((chunks, 2, size, EDGE, samples), jnp.bfloat16),
            pltpu.VMEM(basis.shape, jnp.bfloat16),
            pltpu.VMEM(smooth.shape, jnp.bfloat16),
            pltpu.VMEM((segs, channels), jnp.int32),
            pltpu.VMEM((segs // 2, rows, 2 * channels), jnp.float32),
            edges, edges, edges, edges,
            pltpu.VMEM((2 * channels, 2 * channels), jnp.bfloat16),
            pltpu.VMEM((segs, channels), jnp.float32),
            pltpu.VMEM((rows * size, channels), jnp.float32),
            pltpu.VMEM(block.shape, jnp.bfloat16),
            dma((segs // 2,)),
            dma((2 * chunks,)),
            dma((4,)),
            dma((2, chunks)),
            dma((2, chunks)),
            dma((chunks, shares)),
            dma((chunks, shares)),
            dma((chunks, shares)),
            dma((chunks, shares)),
            dma((chunks,)),
        ],
        compiler_params=pltpu.CompilerParams(
            collective_id=0, has_side_effects=True, vmem_limit_bytes=VMEM_LIMIT
        ),
        name="spectra",
    )(
        *(
            pltpu.with_memory_space_constraint(x, pltpu.HBM)
            for x in (fir_taps, raw_strain, good_mask, jnp.asarray(basis), jnp.asarray(smooth))
        ),
    )

    bins = NF // shares
    step_bins = next(n for n in (12, 9, 6, 4, 3, 2, 1) if bins % n == 0)
    out = pl.pallas_call(
        functools.partial(cross_kernel, step_bins),
        grid=(bins // step_bins,),
        out_shape=jax.ShapeDtypeStruct((bins, 2 * channels, LAGS), jnp.float32),
        in_specs=[vmem] * 4,
        out_specs=pl.BlockSpec((step_bins, 2 * channels, LAGS), lambda i: (i, 0, 0)),
        scratch_shapes=[pltpu.VMEM((channels, LAGS), jnp.float32)],
        compiler_params=pltpu.CompilerParams(vmem_limit_bytes=VMEM_LIMIT),
        name="cross",
    )(*spectral)
    return out.reshape(bins, channels, 2, LAGS)


def solution(mesh):
    return jax.shard_map(
        on_device,
        mesh=mesh,
        in_specs=(P("seg", "fiber", None), P(), P("seg", "fiber")),
        out_specs=P("seg", "fiber", None, None),
        check_vma=False,
    )
```

profile of v0, /device:TPU:0, one launch (start us, length us, event | category | flops | bytes accessed | tf_op | source)
XLA Modules:
  0.0 44.9 jit_solution(1872533922577929855)
XLA Ops:
  0.0 39.9 %spectra.1 = (bf16[4,2,73,8,128]{4,3,2,1,0:T(8,128)(2,1)S(1)}, bf16[4,2,73,8,128]{4,3,2,1,0:T(8,128)(2,1)S(1)}, f32[36,128,256]{2,1,0:T(8,128)S(1)}, bf16[36,128,128]{2,1,0:T(8,128)(2,1)S(1)}) custom-call(f32[31]{0:T(128)} %taps_hbm.1, bf16[16,128,2048]{2,1,0:T(8,128)(2,1)} %raw_ref.1, s32[16,128]{1,0:T(8,128)} %mask_ref.1, ...), custom_call_target="tpu_custom_call" | custom-call | tf_op jit(solution)/shard_map/spectra/pallas_call | solution.py:400
  39.9 5.0 %cross.1 = f32[36,256,128]{2,1,0:T(8,128)} custom-call(bf16[4,2,73,8,128]{4,3,2,1,0:T(8,128)(2,1)S(1)} %get-tuple-element.9.own_ref, bf16[4,2,73,8,128]{4,3,2,1,0:T(8,128)(2,1)S(1)} %get-tuple-element.10.next_ref, f32[36,128,256]{2,1,0:T(8,128)S(1)} %get-tuple-element.11.part_ref, bf16[36,128,128]{2,1,0:T(8,128)(2,1)S(1)} %get-tuple-element.12.turn_ref), custom_call_target="tpu_custom_call" | custom-call | tf_op jit(solution)/shard_map/cross/pallas_call | solution.py:447
where the time goes:
time: 45.1 us; the launch traced here: 44.9 us
  Pallas kernels  44.9 us (100%)
    pallas_call x1, Pallas kernels, on_device(): pl.pallas_call(functools.partial(spectra_kernel, fibers, shares), out_sha...  39.9 us
    pallas_call x1, Pallas kernels, on_device(): pl.pallas_call(functools.partial(cross_kernel, step_bins), grid=(bins //...  5.04 us

commit v1 on v0

v1 whole, which is shorter than its diff:
```python
import functools
import math

import jax
import jax.numpy as jnp
import numpy as np
from jax import lax
from jax.experimental import pallas as pl
from jax.experimental.pallas import tpu as pltpu
from jax.sharding import PartitionSpec as P

NF = 144
LOW = 16
SMOOTH = 4
LAGS = 128
EDGE = 16

epsilon = 1e-06
water_share = 0.1
MESH = pl.DeviceIdType.MESH
VMEM_LIMIT = 44 * 2**20
scope = jax.named_scope


def row_bins(shares):
    per = NF // shares
    return np.concatenate([np.tile(np.arange(k * per, (k + 1) * per), 2) for k in range(shares)])


def row_parts(shares):
    per = NF // shares
    return np.tile(np.repeat(np.arange(2), per), shares)


def dft_rows(samples, shares):
    bins, parts = row_bins(shares), row_parts(shares)
    index = ((bins[:, None] + LOW) * np.arange(samples)[None, :]) % samples
    angles = index.astype(np.float64) * (2.0 * math.pi / samples)
    return np.where(parts[:, None] == 0, np.cos(angles), -np.sin(angles)).astype(jnp.bfloat16)


def smooth_rows(shares):
    bins = row_bins(shares)
    return (np.abs(bins[:, None] - bins[None, :]) <= SMOOTH).astype(jnp.bfloat16)


def two_terms(x):
    hi = x.astype(jnp.bfloat16)
    return hi, (x - hi.astype(jnp.float32)).astype(jnp.bfloat16)


def mm(a, b):
    return jnp.dot(a, b, preferred_element_type=jnp.float32)


def mm_t(a, b):
    return lax.dot_general(a, b, (((1,), (1,)), ((), ())), preferred_element_type=jnp.float32)


def turned(x, shift):
    return pltpu.roll(x, shift, 1) if shift else x


def partner(seg, m):
    bit = 1
    while bit <= m:
        if m & bit:
            seg = seg + bit - 2 * bit * (seg // bit % 2)
        bit *= 2
    return seg


def taken(ref, part, q):
    blocks, _, _, size, channels = ref.shape
    return ref[:, part, q].reshape(blocks * size, channels)


def bin_groups(bins):
    unit = bins // 12
    sizes = [3 * unit, 3 * unit, 3 * unit, 2 * unit, unit] if bins % 12 == 0 else [bins]
    starts = [sum(sizes[:i]) for i in range(len(sizes))]
    return list(zip(starts, sizes))


def late_blocks(shares, chunks):
    blocks = [(chunks - 1, m) for m in range(1, shares) if 2 * m >= shares]
    return blocks + [(c, shares - 1) for c in range(chunks - 2, chunks - 1) if c >= 0]


def next_messages(shares, chunks, bins):
    late = late_blocks(shares, chunks)
    early = [(c, m) for c in range(chunks) for m in range(shares) if (c, m) not in late]
    return [(c, m, 0, bins, 0) for c, m in early] + [
        (c, m, lo, n, 1 + g) for g, (lo, n) in enumerate(bin_groups(bins)) for c, m in late
    ]


def right_side(ref, q):
    re, im = taken(ref, 0, q), taken(ref, 1, q)
    return jnp.concatenate(
        [jnp.concatenate([re, im], axis=1), jnp.concatenate([im, -re], axis=1)], axis=0
    )


def lagged(near, far):
    row = lax.broadcasted_iota(jnp.int32, near.shape, 0)
    col = lax.broadcasted_iota(jnp.int32, near.shape, 1)
    chosen = jnp.where(col > row, near, far)
    return jnp.take_along_axis(chosen, (col + row + 1) % near.shape[0], axis=1)


def cross_bin(f, next_ref, part_ref, turn_ref, scale_v, out_ref, at):
    channels = next_ref.shape[-1]
    far = mm(turn_ref[at], right_side(next_ref, f))
    for n in range(2):
        cells = slice(n * channels, (n + 1) * channels)
        out_ref[at, pl.ds(n, channels, 2), :] = (
            lagged(part_ref[at, :, cells], far[:, cells]) * scale_v[...]
        )


def each_bin(body, lo, count):
    group = next(n for n in (6, 4, 3, 2, 1) if count % n == 0)

    def step(i, carry):
        for b in range(group):
            body(lo + i * group + b)
        return carry

    lax.fori_loop(0, count // group, step, 0)


def spectra_kernel(
    fibers, shares, messages, taps_hbm, raw_ref, mask_ref, basis_hbm, smooth_hbm,
    out_ref, next_ref, part_tail, turn_tail, scale_v,
    own_ref, part_ref, turn_ref, own_flags, next_flags,
    taps_ref, raw_v, edge_v, basis_ref, smooth_ref, flag_v, spec_v, out_l, out_r, in_l, in_r, band_v, mask_v,
    white_v, send_v, send_flags,
    raw_sem, edge_sem, misc_sem, halo_send, halo_recv, own_send, own_recv, next_send, next_recv, local_sem,
    flag_sem,
):
    fib = lax.axis_index("fiber")
    seg = lax.axis_index("seg")
    segs, channels, _ = raw_ref.shape
    rows = basis_ref.shape[0]
    per = rows // shares
    bins = per // 2
    taps = taps_ref.shape[0]
    half = (taps - 1) // 2
    has_prev = fib > 0
    has_next = fib < fibers - 1
    prev = jnp.maximum(fib - 1, 0)
    following = jnp.minimum(fib + 1, fibers - 1)
    size = channels // EDGE
    chunks = segs // size
    groups = bin_groups(bins)
    pairs = segs // 2
    chunk_pairs = size // 2

    taps_copy = pltpu.make_async_copy(taps_hbm, taps_ref, misc_sem.at[3])
    taps_copy.start()
    basis_copy = pltpu.make_async_copy(basis_hbm, basis_ref, misc_sem.at[0])
    basis_copy.start()
    edge_copies = [
        [
            pltpu.make_async_copy(
                raw_ref.at[pl.ds(c * size, size), pl.ds(start, EDGE), :],
                edge_v.at[c, i], edge_sem.at[c],
            )
            for i, start in enumerate((0, channels - EDGE))
        ]
        for c in range(chunks)
    ]
    for copies in edge_copies:
        for copy in copies:
            copy.start()
    mask_copy = pltpu.make_async_copy(mask_ref, flag_v, misc_sem.at[2])
    mask_copy.start()
    smooth_copy = pltpu.make_async_copy(smooth_hbm, smooth_ref, misc_sem.at[1])
    raw_copies = [
        pltpu.make_async_copy(raw_ref.at[pl.ds(2 * p, 2)], raw_v.at[p], raw_sem.at[p])
        for p in range(pairs)
    ]

    barrier = pltpu.get_barrier_semaphore()
    for m in range(1, shares):
        pl.semaphore_signal(
            barrier, inc=1, device_id=(fib, partner(seg, m)), device_id_type=MESH
        )
    @pl.when(has_prev)
    def _():
        pl.semaphore_signal(barrier, inc=1, device_id=(fib - 1, seg), device_id_type=MESH)
    @pl.when(has_next)
    def _():
        pl.semaphore_signal(barrier, inc=1, device_id=(fib + 1, seg), device_id_type=MESH)

    row = lax.broadcasted_iota(jnp.int32, (2 * channels, channels), 0)
    col = lax.broadcasted_iota(jnp.int32, (2 * channels, channels), 1)
    left = row - channels - EDGE
    right = row - EDGE
    place = jnp.where(row < channels, row, jnp.where(left < 0, left, right))
    place = jnp.where(row < channels + 2 * EDGE, place, 8 * channels)
    tap = place - col + half
    band = jnp.zeros((2 * channels, channels), jnp.float32)
    taps_copy.wait()
    for j in range(taps):
        band = jnp.where(tap == j, taps_ref[j], band)
    band_hi, band_lo = two_terms(band)
    band_v[:, :channels] = band_hi
    band_v[:, channels:] = band_lo

    for copy in raw_copies[:chunk_pairs]:
        copy.start()
    smooth_copy.start()

    @pl.when(jnp.logical_not(has_prev))
    def _():
        in_l[...] = jnp.zeros_like(in_l)
    @pl.when(jnp.logical_not(has_next))
    def _():
        in_r[...] = jnp.zeros_like(in_r)
        next_flags[...] = jnp.zeros_like(next_flags)

    def transform_edges(c):
        pltpu.make_async_copy(edge_v.at[c], edge_v.at[c], edge_sem.at[c]).wait()
        ends = mm_t(basis_ref[...], edge_v[c].reshape(2 * channels, -1)).astype(jnp.bfloat16)
        out_l[c] = ends[:, :channels]
        out_r[c] = ends[:, channels:]

    to_prev = [
        pltpu.make_async_remote_copy(
            src_ref=out_l.at[c], dst_ref=in_r.at[c],
            send_sem=halo_send.at[0], recv_sem=halo_recv.at[0, c],
            device_id=(prev, seg), device_id_type=MESH,
        )
        for c in range(chunks)
    ]
    to_next = [
        pltpu.make_async_remote_copy(
            src_ref=out_r.at[c], dst_ref=in_l.at[c],
            send_sem=halo_send.at[1], recv_sem=halo_recv.at[1, c],
            device_id=(following, seg), device_id_type=MESH,
        )
        for c in range(chunks)
    ]
    def send_edges(c):
        @pl.when(has_prev)
        def _():
            to_prev[c].start()
        @pl.when(has_next)
        def _():
            to_next[c].start()

    def waiting_for(area, send_sem, recv_sem):
        return pltpu.make_async_remote_copy(
            src_ref=area, dst_ref=area, send_sem=send_sem, recv_sem=recv_sem,
            device_id=(prev, seg), device_id_type=MESH,
        )

    def flags_own(m):
        return pltpu.make_async_remote_copy(
            src_ref=send_flags, dst_ref=own_flags.at[seg],
            send_sem=flag_sem.at[0], recv_sem=flag_sem.at[1],
            device_id=(fib, partner(seg, m)), device_id_type=MESH,
        )

    all_flags = waiting_for(own_flags.at[pl.ds(0, shares - 1)], flag_sem.at[0], flag_sem.at[1])

    def flags_next():
        return pltpu.make_async_remote_copy(
            src_ref=own_flags, dst_ref=next_flags,
            send_sem=flag_sem.at[2], recv_sem=flag_sem.at[3],
            device_id=(prev, seg), device_id_type=MESH,
        )

    sides = (fib + fibers - 1) // fibers + (2 * fibers - 2 - fib) // fibers
    with scope("basiswait"):
        basis_copy.wait()
    for c in range(chunks):
        with scope(f"edges{c}"):
            transform_edges(c)
        if c == 0:
            with scope("barrier"):
                pl.semaphore_wait(barrier, shares - 1 + sides)
            send_edges(c)
    for copy in raw_copies[chunk_pairs:]:
        copy.start()

    mask_copy.wait()
    mask_v[...] = flag_v[...].astype(jnp.float32)
    send_flags[...] = mask_v[...].astype(jnp.bfloat16)
    own_flags[seg] = mask_v[...].astype(jnp.bfloat16)
    for m in range(1, shares):
        flags_own(m).start()

    lane = lax.broadcasted_iota(jnp.int32, (rows, channels), 1)

    def transform(p):
        raw_copies[p].wait()
        spec_v[p] = mm_t(basis_ref[...], raw_v[p].reshape(2 * channels, -1))

    def whiten_pair(c, i):
        p = c * chunk_pairs + i
        lefts = in_l[c].astype(jnp.float32)
        rights = in_r[c].astype(jnp.float32)
        parts = []
        for h in range(2):
            slot = 2 * i + h
            l_roll = (channels - slot * EDGE) % channels
            r_roll = (channels + EDGE - slot * EDGE) % channels
            edges = jnp.where(lane < EDGE, turned(lefts, l_roll), turned(rights, r_roll))
            hi, lo = two_terms(spec_v[p, :, h * channels : (h + 1) * channels])
            wide = mm(jnp.concatenate([hi, edges.astype(jnp.bfloat16)], axis=1), band_v[...])
            parts.append(
                wide[:, :channels] + wide[:, channels:] + mm(lo, band_v[:channels, :channels])
            )
        filtered = jnp.concatenate(parts, axis=1)
        power = filtered * filtered
        smooth = mm(smooth_ref[...], power.astype(jnp.bfloat16))
        total = jnp.sum(power, axis=0, keepdims=True)
        level = smooth * (1.0 / (2 * SMOOTH + 1)) + (total * (water_share / NF) + epsilon)
        good = jnp.concatenate(
            [mask_v[pl.ds(2 * p, 1), :], mask_v[pl.ds(2 * p + 1, 1), :]], axis=1
        )
        white = filtered * (lax.rsqrt(level) * good)
        white_v[pl.ds(2 * i, rows, size), :] = white[:, :channels]
        white_v[pl.ds(2 * i + 1, rows, size), :] = white[:, channels:]

    def whiten(c):
        for i in range(chunk_pairs):
            whiten_pair(c, i)
        for k in range(shares):
            send_v[c * shares + k] = (
                white_v[k * per * size : (k + 1) * per * size, :]
                .reshape(2, bins, size, channels)
                .astype(jnp.bfloat16)
            )

    def to_own(c, m):
        other = partner(seg, m)
        return pltpu.make_async_remote_copy(
            src_ref=send_v.at[c * shares + other], dst_ref=own_ref.at[c * shares + seg],
            send_sem=own_send.at[0], recv_sem=own_recv.at[c, m],
            device_id=(fib, other), device_id_type=MESH,
        )

    def from_own(c, m):
        other = partner(seg, m)
        return pltpu.make_async_remote_copy(
            src_ref=send_v.at[c * shares + other], dst_ref=own_ref.at[c * shares + other],
            send_sem=own_send.at[0], recv_sem=own_recv.at[c, m],
            device_id=(fib, other), device_id_type=MESH,
        )

    def hand_on(message):
        c, m, lo, count, k = message
        source = c * shares + partner(seg, m)
        block = send_v if m == 0 else own_ref
        return pltpu.make_async_remote_copy(
            src_ref=block.at[source, :, pl.ds(lo, count)],
            dst_ref=next_ref.at[source, :, pl.ds(lo, count)],
            send_sem=next_send.at[0], recv_sem=next_recv.at[k],
            device_id=(prev, seg), device_id_type=MESH,
        )

    def hand_all(*blocks):
        @pl.when(has_prev)
        def _():
            for message in messages:
                if message[:2] in blocks:
                    hand_on(message).start()

    def kept(c):
        mine = c * shares + seg
        return pltpu.make_async_copy(send_v.at[mine], own_ref.at[mine], local_sem.at[0])

    def give(c):
        for m in reversed(range(1, shares)):
            to_own(c, m).start()
        hand_all((c, 0))
        kept(c).start()

    def relay(*blocks):
        for c, m in blocks:
            from_own(c, m).wait_recv()
        hand_all(*blocks)

    def own_bin(f, part, turn, at):
        turned_left = jnp.concatenate([taken(own_ref, 0, f), taken(own_ref, 1, f)], axis=0).T
        turn[at] = turned_left
        part[at] = mm(turned_left, right_side(own_ref, f))

    def grams(a, b):
        return lax.dot_general(a, b, (((0,), (0,)), ((), ())), preferred_element_type=jnp.float32)

    smooth_copy.wait()
    for c in range(chunks):
        for i in range(chunk_pairs):
            with scope(f"transform{c}{i}"):
                transform(c * chunk_pairs + i)
            if c + 1 < chunks and i == 2:
                send_edges(c + 1)
            if c and i == chunk_pairs // 2:
                with scope(f"relayin{c}"):
                    relay((c - 1, 1))
        with scope(f"halowait{c}"):
            @pl.when(has_prev)
            def _():
                to_next[c].wait_recv()
            @pl.when(has_next)
            def _():
                to_prev[c].wait_recv()
        with scope(f"whiten{c}"):
            whiten(c)
        with scope(f"give{c}"):
            give(c)

    @pl.when(jnp.logical_not(has_next))
    def _():
        next_ref[...] = jnp.zeros_like(next_ref)

    with scope("flags"):
        all_flags.wait_recv()
        @pl.when(has_prev)
        def _():
            flags_next().start()

    late = late_blocks(shares, chunks)
    early = [(chunks - 1, 1)] + [(c, m) for c in range(chunks) for m in range(2, shares)]
    for c, m in early:
        if (c, m) not in late:
            with scope(f"relay{c}{m}"):
                relay((c, m))
    with scope("relaylate"):
        relay(*late)
    given = send_v.at[pl.ds(0, chunks)]
    pltpu.make_async_copy(given, given, local_sem.at[0]).wait()

    with scope("ownprod"):
        tail, count = groups[-1]
        each_bin(lambda f: own_bin(f, part_ref, turn_ref, f), 0, tail)
        for f in range(count):
            own_bin(tail + f, part_tail, turn_tail, f)

    with scope("scale"):
        @pl.when(has_next)
        def _():
            flags_next().wait_recv()
        here = own_flags[...].reshape(shares * segs, channels)
        there = next_flags[...].reshape(shares * segs, channels)
        scale_v[...] = 1.0 / jnp.maximum(lagged(grams(here, here), grams(here, there)), 1.0)

    for g, (lo, count) in enumerate(groups):
        with scope(f"recv{lo}"):
            @pl.when(has_next)
            def _():
                if g == 0:
                    whole = next_ref.at[pl.ds(0, shares * chunks - len(late))]
                    waiting_for(whole, next_send.at[0], next_recv.at[0]).wait_recv()
                area = next_ref.at[pl.ds(0, len(late)), :, pl.ds(lo, count)]
                waiting_for(area, next_send.at[0], next_recv.at[1 + g]).wait_recv()
        if g + 1 < len(groups):
            with scope(f"cross{lo}"):
                each_bin(
                    lambda f: cross_bin(f, next_ref, part_ref, turn_ref, scale_v, out_ref, f), lo, count
                )

    all_flags.wait_send()
    waiting_for(
        send_v.at[pl.ds(0, chunks * (shares - 1))], own_send.at[0], own_recv.at[0, 0]
    ).wait_send()
    @pl.when(has_prev)
    def _():
        flags_next().wait_send()
        waiting_for(out_l, halo_send.at[0], halo_recv.at[0, 0]).wait_send()
        waiting_for(own_ref, next_send.at[0], next_recv.at[0]).wait_send()
    @pl.when(has_next)
    def _():
        waiting_for(out_r, halo_send.at[1], halo_recv.at[1, 0]).wait_send()


def finish_kernel(done_ref, next_ref, part_tail, turn_tail, scale_v, out_ref, last_v, sem):
    bins = done_ref.shape[0]
    lo, count = bin_groups(bins)[-1]
    copies = [
        pltpu.make_async_copy(done_ref.at[pl.ds(a, n)], out_ref.at[pl.ds(a, n)], sem.at[i])
        for i, (a, n) in enumerate(bin_groups(bins)[:-1])
    ]
    for copy in copies:
        copy.start()
    for i in range(count):
        cross_bin(lo + i, next_ref, part_tail, turn_tail, scale_v, last_v, i)
    copies.append(
        pltpu.make_async_copy(last_v, out_ref.at[pl.ds(lo, count)], sem.at[len(copies)])
    )
    copies[-1].start()
    for copy in copies:
        copy.wait()


def on_device(raw_strain, fir_taps, good_mask):
    segs, channels, samples = raw_strain.shape
    fibers, shares = lax.axis_size("fiber"), lax.axis_size("seg")
    rows = 2 * NF
    per = rows // shares
    bins = per // 2
    size = channels // EDGE
    chunks = segs // size
    shape = (shares * chunks, 2, bins, size, channels)
    block = pltpu.VMEM(shape, jnp.bfloat16)
    flags = pltpu.VMEM((shares, segs, channels), jnp.bfloat16)
    vmem = pl.BlockSpec(memory_space=pltpu.VMEM)
    hbm = pl.BlockSpec(memory_space=pltpu.HBM)
    edges = pltpu.VMEM((chunks, rows, size * EDGE), jnp.bfloat16)
    basis, smooth = dft_rows(samples, shares), smooth_rows(shares)
    dma = pltpu.SemaphoreType.DMA
    messages = next_messages(shares, chunks, bins)
    count = bin_groups(bins)[-1][1]
    whole = jax.ShapeDtypeStruct((bins, 2 * channels, LAGS), jnp.float32)
    crossed = pl.pallas_call(
        functools.partial(spectra_kernel, fibers, shares, messages),
        out_shape=(
            whole,
            jax.ShapeDtypeStruct(shape, jnp.bfloat16),
            jax.ShapeDtypeStruct((count, channels, 2 * channels), jnp.float32),
            jax.ShapeDtypeStruct((count, channels, 2 * shares * segs), jnp.bfloat16),
            jax.ShapeDtypeStruct((channels, LAGS), jnp.float32),
        ),
        in_specs=[hbm] * 5,
        out_specs=(vmem,) * 5,
        scratch_shapes=[
            block,
            pltpu.VMEM((bins - count, channels, 2 * channels), jnp.float32),
            pltpu.VMEM((bins - count, channels, 2 * shares * segs), jnp.bfloat16),
            flags,
            flags,
            pltpu.SMEM(fir_taps.shape, jnp.float32),
            pltpu.VMEM((segs // 2, 2, channels, samples), jnp.bfloat16),
            pltpu.VMEM((chunks, 2, size, EDGE, samples), jnp.bfloat16),
            pltpu.VMEM(basis.shape, jnp.bfloat16),
            pltpu.VMEM(smooth.shape, jnp.bfloat16),
            pltpu.VMEM((segs, channels), jnp.int32),
            pltpu.VMEM((segs // 2, rows, 2 * channels), jnp.float32),
            edges, edges, edges, edges,
            pltpu.VMEM((2 * channels, 2 * channels), jnp.bfloat16),
            pltpu.VMEM((segs, channels), jnp.float32),
            pltpu.VMEM((rows * size, channels), jnp.float32),
            block,
            pltpu.VMEM((segs, channels), jnp.bfloat16),
            dma((segs // 2,)),
            dma((chunks,)),
            dma((4,)),
            dma((2,)),
            dma((2, chunks)),
            dma((1,)),
            dma((chunks, shares)),
            dma((1,)),
            dma((1 + len(bin_groups(bins)),)),
            dma((1,)),
            dma((4,)),
        ],
        compiler_params=pltpu.CompilerParams(
            collective_id=0, has_side_effects=True, vmem_limit_bytes=VMEM_LIMIT
        ),
        name="spectra",
    )(
        *(
            pltpu.with_memory_space_constraint(x, pltpu.HBM)
            for x in (fir_taps, raw_strain, good_mask, jnp.asarray(basis), jnp.asarray(smooth))
        ),
    )
    out = pl.pallas_call(
        finish_kernel,
        out_shape=whole,
        in_specs=[vmem] * 5,
        out_specs=hbm,
        scratch_shapes=[
            pltpu.VMEM((count, 2 * channels, LAGS), jnp.float32),
            dma((len(bin_groups(bins)),)),
        ],
        compiler_params=pltpu.CompilerParams(vmem_limit_bytes=VMEM_LIMIT),
        name="finish",
    )(*crossed)
    return out.reshape(bins, channels, 2, LAGS)


def solution(mesh):
    return jax.shard_map(
        on_device,
        mesh=mesh,
        in_specs=(P("seg", "fiber", None), P(), P("seg", "fiber")),
        out_specs=P("seg", "fiber", None, None),
        check_vma=False,
    )
```

time: 45.1 us -> 40.2 us (0.89)
  Pallas kernels: 44.9 us -> 40 us
    pallas_call x2, Pallas kernels: 44.9 us -> 40 us  [the longest x1 37.8 us: on_device(): pl.pallas_call(functools.partial(spectra_kernel, fibers, shares, messages...]
where the time goes in v1:
time: 40.2 us; the launch traced here: 40 us
  Pallas kernels  40 us (100%)
    pallas_call x1, Pallas kernels, on_device(): pl.pallas_call(functools.partial(spectra_kernel, fibers, shares, messages...  37.8 us
    pallas_call x1, Pallas kernels, on_device(): pl.pallas_call(finish_kernel, out_shape=whole, in_specs=[vmem] * 5, out_s...  2.22 us

profile of v1, /device:TPU:0, one launch (start us, length us, event | category | flops | bytes accessed | tf_op | source)
XLA Modules:
  0.0 40.0 jit_solution(13218973141929707176)
XLA Ops:
  0.0 37.8 %spectra.1 = (f32[36,256,128]{2,1,0:T(8,128)S(1)}, bf16[8,2,36,8,128]{4,3,2,1,0:T(8,128)(2,1)S(1)}, f32[3,128,256]{2,1,0:T(8,128)S(1)}, bf16[3,128,128]{2,1,0:T(8,128)(2,1)S(1)}, f32[128,128]{1,0:T(8,128)S(1)}) custom-call(f32[31]{0:T(128)} %taps_hbm.1, bf16[16,128,2048]{2,1,0:T(8,128)(2,1)} %raw_ref.1, s32[16,128]{1,0:T(8,128)} %mask_ref.1, ...), custom_call_target="tpu_custom_call" | custom-call | tf_op jit(solution)/shard_map/spectra/pallas_call | solution.py:520
  37.8 2.2 %finish.1 = f32[36,256,128]{2,1,0:T(8,128)} custom-call(f32[36,256,128]{2,1,0:T(8,128)S(1)} %get-tuple-element.10.done_ref, bf16[8,2,36,8,128]{4,3,2,1,0:T(8,128)(2,1)S(1)} %get-tuple-element.11.next_ref, f32[3,128,256]{2,1,0:T(8,128)S(1)} %get-tuple-element.12.part_tail, bf16[3,128,128]{2,1,0:T(8,128)(2,1)S(1)} %get-tuple-element.13.turn_tail, ...), custom_call_target="tpu_custom_call" | custom-call | tf_op jit(solution)/shard_map/finish/pallas_call | solution.py:572

commit v2 on v1

--- a/solution.py
+++ b/solution.py
@@ -134,7 +134,7 @@
     fibers, shares, messages, taps_hbm, raw_ref, mask_ref, basis_hbm, smooth_hbm,
     out_ref, next_ref, part_tail, turn_tail, scale_v,
     own_ref, part_ref, turn_ref, own_flags, next_flags,
-    taps_ref, raw_v, edge_v, basis_ref, smooth_ref, flag_v, spec_v, out_l, out_r, in_l, in_r, band_v, mask_v,
+    taps_ref, raw_v, edge_v, basis_ref, smooth_ref, flag_v, spec_v, out_l, out_r, in_l, in_r, band_v, ends_v, mask_v,
     white_v, send_v, send_flags,
     raw_sem, edge_sem, misc_sem, halo_send, halo_recv, own_send, own_recv, next_send, next_recv, local_sem,
     flag_sem,
@@ -206,8 +206,12 @@
     for j in range(taps):
         band = jnp.where(tap == j, taps_ref[j], band)
     band_hi, band_lo = two_terms(band)
-    band_v[:, :channels] = band_hi
-    band_v[:, channels:] = band_lo
+    band_v[:channels, :channels] = band_hi[:channels]
+    band_v[:channels, channels:] = band_lo[:channels]
+    band_v[channels:, :channels] = band_hi[:channels]
+    band_v[channels:, channels:] = jnp.zeros_like(band_lo[:channels])
+    ends_v[:, :channels] = band_hi[channels:]
+    ends_v[:, channels:] = band_lo[channels:]
 
     for copy in raw_copies[:chunk_pairs]:
         copy.start()
@@ -299,6 +303,12 @@
         raw_copies[p].wait()
         spec_v[p] = mm_t(basis_ref[...], raw_v[p].reshape(2 * channels, -1))
 
+    def filter_pair(p):
+        for h in range(2):
+            cells = slice(h * channels, (h + 1) * channels)
+            wide = mm(jnp.concatenate(two_terms(spec_v[p, :, cells]), axis=1), band_v[...])
+            spec_v[p, :, cells] = wide[:, :channels] + wide[:, channels:]
+
     def whiten_pair(c, i):
         p = c * chunk_pairs + i
         lefts = in_l[c].astype(jnp.float32)
@@ -309,11 +319,9 @@
             l_roll = (channels - slot * EDGE) % channels
             r_roll = (channels + EDGE - slot * EDGE) % channels
             edges = jnp.where(lane < EDGE, turned(lefts, l_roll), turned(rights, r_roll))
-            hi, lo = two_terms(spec_v[p, :, h * channels : (h + 1) * channels])
-            wide = mm(jnp.concatenate([hi, edges.astype(jnp.bfloat16)], axis=1), band_v[...])
-            parts.append(
-                wide[:, :channels] + wide[:, channels:] + mm(lo, band_v[:channels, :channels])
-            )
+            wide = mm(edges.astype(jnp.bfloat16), ends_v[...])
+            inner = spec_v[p, :, h * channels : (h + 1) * channels]
+            parts.append(inner + (wide[:, :channels] + wide[:, channels:]))
         filtered = jnp.concatenate(parts, axis=1)
         power = filtered * filtered
         smooth = mm(smooth_ref[...], power.astype(jnp.bfloat16))
@@ -403,6 +411,9 @@
             if c and i == chunk_pairs // 2:
                 with scope(f"relayin{c}"):
                     relay((c - 1, 1))
+        with scope(f"filter{c}"):
+            for i in range(chunk_pairs):
+                filter_pair(c * chunk_pairs + i)
         with scope(f"halowait{c}"):
             @pl.when(has_prev)
             def _():
@@ -543,6 +554,7 @@
             pltpu.VMEM((segs // 2, rows, 2 * channels), jnp.float32),
             edges, edges, edges, edges,
             pltpu.VMEM((2 * channels, 2 * channels), jnp.bfloat16),
+            pltpu.VMEM((channels, 2 * channels), jnp.bfloat16),
             pltpu.VMEM((segs, channels), jnp.float32),
             pltpu.VMEM((rows * size, channels), jnp.float32),
             block,

time: 40.2 us -> 40 us (level)
  no operation moved by 1% of the time
where the time goes in v2:
time: 40 us; the launch traced here: 39.9 us
  Pallas kernels  39.8 us (99%)
    pallas_call x1, Pallas kernels, on_device(): pl.pallas_call(functools.partial(spectra_kernel, fibers, shares, messages...  37.6 us
    pallas_call x1, Pallas kernels, on_device(): pl.pallas_call(finish_kernel, out_shape=whole, in_specs=[vmem] * 5, out_s...  2.22 us

profile of v2, /device:TPU:0, one launch (start us, length us, event | category | flops | bytes accessed | tf_op | source)
XLA Modules:
  0.0 39.9 jit_solution(5427233797027108649)
XLA Ops:
  0.0 37.6 %spectra.1 = (f32[36,256,128]{2,1,0:T(8,128)S(1)}, bf16[8,2,36,8,128]{4,3,2,1,0:T(8,128)(2,1)S(1)}, f32[3,128,256]{2,1,0:T(8,128)S(1)}, bf16[3,128,128]{2,1,0:T(8,128)(2,1)S(1)}, f32[128,128]{1,0:T(8,128)S(1)}) custom-call(f32[31]{0:T(128)} %taps_hbm.1, bf16[16,128,2048]{2,1,0:T(8,128)(2,1)} %raw_ref.1, s32[16,128]{1,0:T(8,128)} %mask_ref.1, ...), custom_call_target="tpu_custom_call" | custom-call | tf_op jit(solution)/shard_map/spectra/pallas_call | solution.py:531
  37.6 2.2 %finish.1 = f32[36,256,128]{2,1,0:T(8,128)} custom-call(f32[36,256,128]{2,1,0:T(8,128)S(1)} %get-tuple-element.10.done_ref, bf16[8,2,36,8,128]{4,3,2,1,0:T(8,128)(2,1)S(1)} %get-tuple-element.11.next_ref, f32[3,128,256]{2,1,0:T(8,128)S(1)} %get-tuple-element.12.part_tail, bf16[3,128,128]{2,1,0:T(8,128)(2,1)S(1)} %get-tuple-element.13.turn_tail, ...), custom_call_target="tpu_custom_call" | custom-call | tf_op jit(solution)/shard_map/finish/pallas_call | solution.py:584
